TPU v7x, 32 devices: a whole 2x2x4 slice. The times are simulated.
32 devices in a mesh: tm: 4 (over x, core), pair: 8 (over z, y).
Axes of the slice: x: 2, y: 2, z: 4, core: 2. Of those that a mesh axis runs over, the one named last changes fastest.
Arguments:
- orbitals: bfloat16 [8192, 512], P('pair', 'tm'), may hold values from -1.5 to 1.5
- level_gap: float32 [512], replicated, may hold values from 0.05 to 1.5
- screened: bfloat16 [8, 32, 1024, 1024], P('tm', 'pair'), may hold values from -0.008972168 to 0.008972168
- pair_blocks: int32 [32, 2], P('pair'), may hold values from 0 to 7, as said below
Outputs:
- self_energy: float32 [8, 512, 512], P('tm', 'pair')
Inputs may be any that keep to these rules, and one draw needn't show every extreme that they name: `pair_blocks`: each row names two point blocks a <= c; no unordered pair appears in two rows; the pair (0, 7) appears in every draw.
All inputs are finite; a program needn't handle non-finite values.
Results may differ from a plain program's by a relative error of at most 0.0049.
Values may be sent and summed in bfloat16 or wider, within the bound.
A program may use at most 128 MiB of HBM per device.

v0:
```python
import jax
import jax.numpy as jnp
from jax import lax
from jax.sharding import PartitionSpec as P

NOCC = 128


def shards(orbitals, level_gap, screened, pair_blocks):
    block_rows = orbitals.shape[0]
    wanted = pair_blocks.reshape(-1)
    narrow = lax.all_gather(orbitals, "pair", axis=0, tiled=True)
    picked = jnp.take(narrow.reshape(-1, block_rows, narrow.shape[1]), wanted, axis=0)
    chosen = lax.all_gather(picked, "tm", axis=2, tiled=True)
    orbital_count = chosen.shape[2]
    time_local = screened.shape[0]
    pair_local = screened.shape[1]
    time_total = time_local * lax.axis_size("tm")
    first_time = lax.axis_index("tm") * time_local
    moments = (first_time + jnp.arange(time_local)).astype(jnp.float32)
    tau = 6.0 * (moments + 0.5) / time_total
    signs = jnp.where(jnp.arange(orbital_count) < NOCC, 1.0, -1.0).astype(jnp.float32)
    factors = signs[None, :] * jnp.exp(-level_gap[None, :] * tau[:, None])
    totals = []
    for time_step in range(time_local):
        total = jnp.zeros((orbital_count, orbital_count), jnp.float32)
        for pair_step in range(pair_local):
            left = chosen[2 * pair_step]
            right = chosen[2 * pair_step + 1]
            scaled = (left.astype(jnp.float32) * factors[time_step][None, :]).astype(jnp.bfloat16)
            green = lax.dot_general(
                scaled, right, (((1,), (1,)), ((), ())), preferred_element_type=jnp.float32
            )
            product = (green * screened[time_step, pair_step].astype(jnp.float32)).astype(
                jnp.bfloat16
            )
            half = lax.dot_general(
                left, product, (((0,), (0,)), ((), ())), preferred_element_type=jnp.float32
            ).astype(jnp.bfloat16)
            block = jnp.dot(half, right, preferred_element_type=jnp.float32)
            weight = jnp.where(
                pair_blocks[pair_step, 0] == pair_blocks[pair_step, 1], 0.5, 1.0
            ).astype(jnp.float32)
            total = total + weight * (block + block.T)
        totals.append(total)
    partial_sum = jnp.stack(totals, axis=0)
    return lax.psum_scatter(partial_sum, "pair", scatter_dimension=1, tiled=True)


def solution(mesh):
    return jax.shard_map(
        shards,
        mesh=mesh,
        in_specs=(P("pair", "tm"), P(), P("tm", "pair", None, None), P("pair", None)),
        out_specs=P("tm", "pair", None),
        check_vma=False,
    )
```

profile of v0, /device:TPU:0, one launch (start us, length us, event | category | flops | bytes accessed | tf_op | source)
XLA Modules:
  0.0 293.7 jit_solution(13461157398110118424)
XLA Ops:
  6.5 0.0 all-gather.3.cloned.1.call-start
  6.5 0.7 all-gather.3.cloned.1.call-update
  7.3 0.0 all-gather.5.cloned.1.call-start
  7.3 0.8 copy.15
  8.1 0.1 reshape.146
  8.2 0.1 reshape.144
  8.3 53.0 %all-gather.3.cloned.1.call-done = bf16[8192,128]{1,0:T(8,128)(2,1)} async-done(((bf16[1024,128]{1,0:T(8,128)(2,1)}), bf16[8192,128]{1,0:T(8,128)(2,1)}) %all-gather.3.cloned.1.call-update) | async-done | bytes 2097168 | tf_op jit(solution)/shard_map/all_gather | solution.py:12
  61.3 2.5 gather_fusion
  63.8 0.0 copy-start.9
  63.9 0.0 copy-start.8
  63.9 1.7 broadcast_select_fusion
  65.5 0.0 all-gather.5.cloned.1.call-update
  65.5 0.0 reduce-scatter.2.cloned.1.call-start
  65.6 0.0 copy-done.9
  65.6 0.0 copy-done.8
  65.6 0.7 fusion.115
  71.3 0.1 exponential_multiply_fusion
  71.4 52.2 %all-gather.5.cloned.1.call-done = bf16[8,1024,512]{2,1,0:T(8,128)(2,1)} async-done(((bf16[8,1024,128]{2,1,0:T(8,128)(2,1)}), bf16[8,1024,512]{2,1,0:T(8,128)(2,1)}) %all-gather.5.cloned.1.call-update) | async-done | bytes 8388624 | tf_op jit(solution)/shard_map/all_gather | solution.py:14
  123.6 4.9 %convolution_convert_fusion.3 = bf16[512,1024]{1,0:T(8,128)(2,1)S(1)} fusion(bf16[2,4,1024,1024]{3,2,1,0:T(8,128)(2,1)} %param.6, f32[512]{0:T(512)S(1)} %bitcast.218, bf16[8,1024,512]{2,1,0:T(8,128)(2,1)} %all-gather.5.cloned.1.call-done), kind=kOutput, calls=%fused_computation.38 | convolution fusion | flops 2152726528 | bytes 6293504 | tf_op jit(solution)/shard_map/dot_general | solution.py:37
  128.5 1.9 fusion.104
  130.5 0.3 copy.21
  130.8 6.0 %convolution_convert_fusion.2 = bf16[512,1024]{1,0:T(8,128)(2,1)} fusion(bf16[2,4,1024,1024]{3,2,1,0:T(8,128)(2,1)} %param.6, f32[512]{0:T(512)S(1)} %bitcast.219, bf16[8,1024,512]{2,1,0:T(8,128)(2,1)} %all-gather.5.cloned.1.call-done), kind=kOutput, calls=%fused_computation.37 | convolution fusion | flops 2152726528 | bytes 6293504 | tf_op jit(solution)/shard_map/dot_general | solution.py:37
  136.8 2.2 fusion.106
  139.0 1.4 copy.22
  140.4 5.9 %convolution_convert_fusion = bf16[512,1024]{1,0:T(8,128)(2,1)} fusion(bf16[2,4,1024,1024]{3,2,1,0:T(8,128)(2,1)} %param.6, f32[512]{0:T(512)S(1)} %bitcast.220, bf16[8,1024,512]{2,1,0:T(8,128)(2,1)} %all-gather.5.cloned.1.call-done), kind=kOutput, calls=%fused_computation.35 | convolution fusion | flops 2152726528 | bytes 6293504 | tf_op jit(solution)/shard_map/dot_general | solution.py:37
  146.3 3.2 %fusion.110 = f32[512,512]{1,0:T(8,128)} fusion(bf16[512,1024]{1,0:T(8,128)(2,1)} %convolution_convert_fusion, bf16[8,1024,512]{2,1,0:T(8,128)(2,1)} %all-gather.5.cloned.1.call-done), kind=kOutput, calls=%fused_computation.109 | convolution fusion | flops 536870912 | bytes 3145728 | tf_op jit(solution)/shard_map/dot_general | solution.py:40
  149.6 2.5 copy.24
  152.1 6.0 %convolution_convert_fusion.1 = bf16[512,1024]{1,0:T(8,128)(2,1)} fusion(bf16[2,4,1024,1024]{3,2,1,0:T(8,128)(2,1)} %param.6, f32[512]{0:T(512)S(1)} %bitcast.221, bf16[8,1024,512]{2,1,0:T(8,128)(2,1)} %all-gather.5.cloned.1.call-done), kind=kOutput, calls=%fused_computation.36 | convolution fusion | flops 2152726528 | bytes 6293504 | tf_op jit(solution)/shard_map/dot_general | solution.py:37
  158.1 3.2 %fusion.108 = f32[512,512]{1,0:T(8,128)} fusion(bf16[512,1024]{1,0:T(8,128)(2,1)} %convolution_convert_fusion.1, bf16[8,1024,512]{2,1,0:T(8,128)(2,1)} %all-gather.5.cloned.1.call-done), kind=kOutput, calls=%fused_computation.107 | convolution fusion | flops 536870912 | bytes 3145728 | tf_op jit(solution)/shard_map/dot_general | solution.py:40
  161.3 2.6 copy.23
  163.9 6.1 %convolution_convert_fusion.4 = bf16[512,1024]{1,0:T(8,128)(2,1)} fusion(bf16[2,4,1024,1024]{3,2,1,0:T(8,128)(2,1)} %param.6, f32[512]{0:T(512)S(1)} %bitcast.214, bf16[8,1024,512]{2,1,0:T(8,128)(2,1)} %all-gather.5.cloned.1.call-done), kind=kOutput, calls=%fused_computation.39 | convolution fusion | flops 2152726528 | bytes 6293504 | tf_op jit(solution)/shard_map/dot_general | solution.py:37
  170.0 3.2 %fusion.111 = f32[512,512]{1,0:T(8,128)} fusion(bf16[512,1024]{1,0:T(8,128)(2,1)} %convolution_convert_fusion.4, bf16[8,1024,512]{2,1,0:T(8,128)(2,1)} %all-gather.5.cloned.1.call-done), kind=kOutput, calls=%fused_computation.110 | convolution fusion | flops 536870912 | bytes 3145728 | tf_op jit(solution)/shard_map/dot_general | solution.py:40
  173.2 2.5 copy.20
  175.7 5.9 %convolution_convert_fusion.5 = bf16[512,1024]{1,0:T(8,128)(2,1)} fusion(bf16[2,4,1024,1024]{3,2,1,0:T(8,128)(2,1)} %param.6, f32[512]{0:T(512)S(1)} %bitcast.215, bf16[8,1024,512]{2,1,0:T(8,128)(2,1)} %all-gather.5.cloned.1.call-done), kind=kOutput, calls=%fused_computation.40 | convolution fusion | flops 2152726528 | bytes 6293504 | tf_op jit(solution)/shard_map/dot_general | solution.py:37
  181.7 3.2 %fusion.109 = f32[512,512]{1,0:T(8,128)} fusion(bf16[512,1024]{1,0:T(8,128)(2,1)} %convolution_convert_fusion.5, bf16[8,1024,512]{2,1,0:T(8,128)(2,1)} %all-gather.5.cloned.1.call-done), kind=kOutput, calls=%fused_computation.108 | convolution fusion | flops 536870912 | bytes 3145728 | tf_op jit(solution)/shard_map/dot_general | solution.py:40
  184.9 2.5 copy.19
  187.4 5.9 %convolution_convert_fusion.7 = bf16[512,1024]{1,0:T(8,128)(2,1)} fusion(bf16[2,4,1024,1024]{3,2,1,0:T(8,128)(2,1)} %param.6, f32[512]{0:T(512)S(1)} %bitcast.216, bf16[8,1024,512]{2,1,0:T(8,128)(2,1)} %all-gather.5.cloned.1.call-done), kind=kOutput, calls=%fused_computation.42 | convolution fusion | flops 2152726528 | bytes 6293504 | tf_op jit(solution)/shard_map/dot_general | solution.py:37
  193.3 3.2 %fusion.105 = f32[512,512]{1,0:T(8,128)} fusion(bf16[512,1024]{1,0:T(8,128)(2,1)} %convolution_convert_fusion.7, bf16[8,1024,512]{2,1,0:T(8,128)(2,1)} %all-gather.5.cloned.1.call-done), kind=kOutput, calls=%fused_computation.104 | convolution fusion | flops 536870912 | bytes 3145728 | tf_op jit(solution)/shard_map/dot_general | solution.py:40
  196.6 2.5 copy.17
  199.1 5.9 %convolution_convert_fusion.6 = bf16[512,1024]{1,0:T(8,128)(2,1)} fusion(bf16[2,4,1024,1024]{3,2,1,0:T(8,128)(2,1)} %param.6, f32[512]{0:T(512)S(1)} %bitcast.217, bf16[8,1024,512]{2,1,0:T(8,128)(2,1)} %all-gather.5.cloned.1.call-done), kind=kOutput, calls=%fused_computation.41 | convolution fusion | flops 2152726528 | bytes 6293504 | tf_op jit(solution)/shard_map/dot_general | solution.py:37
  205.0 3.3 %fusion.107 = f32[512,512]{1,0:T(8,128)} fusion(bf16[512,1024]{1,0:T(8,128)(2,1)} %convolution_convert_fusion.6, bf16[8,1024,512]{2,1,0:T(8,128)(2,1)} %all-gather.5.cloned.1.call-done), kind=kOutput, calls=%fused_computation.106 | convolution fusion | flops 536870912 | bytes 3145728 | tf_op jit(solution)/shard_map/dot_general | solution.py:40
  208.3 2.5 copy.18
  210.8 0.0 copy-start
  210.8 0.0 copy-start.1
  210.8 0.0 copy-start.2
  210.8 0.0 copy-start.3
  210.8 0.0 copy-start.4
  210.8 0.0 copy-start.5
  210.8 0.0 copy-start.6
  210.8 0.0 copy-start.7
  210.8 3.7 %fusion.34 = f32[1,512,512]{2,1,0:T(8,128)S(1)} fusion(f32[512,512]{1,0:T(8,128)} %fusion.110, f32[512,512]{0,1:T(8,128)} %copy.24, f32[512,512]{1,0:T(8,128)} %fusion.108, f32[512,512]{0,1:T(8,128)} %copy.23, f32[512,512]{1,0:T(8,128)S(1)} %fusion.106, f32[512,512]{0,1:T(8,128)} %copy.22, f32[512,512]{1,0:T(8,128)S(1)} %fusion.104, ...), kind=kLoop, calls=%fused_computation.58 | loop fusion | flops 2883584 | bytes 9437200 | tf_op jit(solution)/shard_map/stack | solution.py:46
  214.6 0.0 copy-done
  214.6 0.0 copy-done.1
  214.6 0.0 copy-done.2
  214.6 0.0 copy-done.3
  214.6 0.2 copy-done.4
  214.9 0.3 copy-done.5
  215.2 0.3 copy-done.6
  215.5 0.3 copy-done.7
  215.8 1.0 fusion.42
  216.8 1.5 pad_maximum_fusion
  218.3 0.0 reduce-scatter.2.cloned.1.call-update
  218.3 68.9 %reduce-scatter.2.cloned.1.call-done = f32[2,64,512]{2,1,0:T(8,128)} async-done(((f32[2,512,512]{2,1,0:T(8,128)}), f32[2,64,512]{2,1,0:T(8,128)}) %reduce-scatter.2.cloned.1.call-update) | async-done | bytes 262160 | tf_op jit(solution)/shard_map/reduce_scatter | solution.py:47
  (7 shorter events, 0.0 us)
Async XLA Ops:
  6.5 54.8 %all-gather.3.cloned.1.call-start = ((), (), s32[]{:S(2)}) async-start(), calls=%async_computation.1 | async-start | bytes 2359296 | tf_op jit(solution)/shard_map/all_gather | solution.py:12
  7.3 116.4 %all-gather.5.cloned.1.call-start = ((), (), s32[]{:S(2)}) async-start(), calls=%async_computation.2 | async-start | bytes 10485760 | tf_op jit(solution)/shard_map/all_gather | solution.py:14
  63.8 1.8 copy-start.9
  63.9 1.8 copy-start.8
  65.5 221.7 %reduce-scatter.2.cloned.1.call-start = ((), (), s32[]{:S(2)}) async-start(), calls=%async_computation.3 | async-start | bytes 2359296 | tf_op jit(solution)/shard_map/reduce_scatter | solution.py:47
  210.8 3.8 %copy-start = (f32[512,512]{1,0:T(8,128)S(1)}, f32[512,512]{1,0:T(8,128)}, u32[]{:S(2)}) copy-start(f32[512,512]{1,0:T(8,128)} %fusion.111) | copy-start | bytes 3145732
  210.8 3.8 %copy-start.1 = (f32[512,512]{0,1:T(8,128)S(1)}, f32[512,512]{0,1:T(8,128)}, u32[]{:S(2)}) copy-start(f32[512,512]{0,1:T(8,128)} %copy.20) | copy-start | bytes 3145732
  210.8 3.8 %copy-start.2 = (f32[512,512]{1,0:T(8,128)S(1)}, f32[512,512]{1,0:T(8,128)}, u32[]{:S(2)}) copy-start(f32[512,512]{1,0:T(8,128)} %fusion.109) | copy-start | bytes 3145732
  210.8 3.8 %copy-start.3 = (f32[512,512]{0,1:T(8,128)S(1)}, f32[512,512]{0,1:T(8,128)}, u32[]{:S(2)}) copy-start(f32[512,512]{0,1:T(8,128)} %copy.19) | copy-start | bytes 3145732
  210.8 4.1 %copy-start.4 = (f32[512,512]{1,0:T(8,128)S(1)}, f32[512,512]{1,0:T(8,128)}, u32[]{:S(2)}) copy-start(f32[512,512]{1,0:T(8,128)} %fusion.105) | copy-start | bytes 3145732
  210.8 4.4 %copy-start.5 = (f32[512,512]{0,1:T(8,128)S(1)}, f32[512,512]{0,1:T(8,128)}, u32[]{:S(2)}) copy-start(f32[512,512]{0,1:T(8,128)} %copy.17) | copy-start | bytes 3145732
  210.8 4.7 %copy-start.6 = (f32[512,512]{1,0:T(8,128)S(1)}, f32[512,512]{1,0:T(8,128)}, u32[]{:S(2)}) copy-start(f32[512,512]{1,0:T(8,128)} %fusion.107) | copy-start | bytes 3145732
  210.8 4.9 %copy-start.7 = (f32[512,512]{0,1:T(8,128)S(1)}, f32[512,512]{0,1:T(8,128)}, u32[]{:S(2)}) copy-start(f32[512,512]{0,1:T(8,128)} %copy.18) | copy-start | bytes 3145732
Sparse Core Ops, SparseCore 0:
  9.5 51.7 all-gather.2
  65.7 57.8 all-gather.4
  218.5 68.6 reduce-scatter.1
where the time goes:
time: 294 us
  waiting for transfers between devices  175 us (60%)
  matrix products  70.1 us (24%)
  local copies, waits for them, and re-layouts  22.4 us (8%)
  between operations  18.3 us (6%)
  other arithmetic  8.04 us (3%)
    reduce_scatter x1, waiting for transfers between devices, shards(): lax.psum_scatter(partial_sum, 'pair', scatter_dimension=1, tiled=True)  68.9 us
    all_gather x1, waiting for transfers between devices, shards(): narrow = lax.all_gather(orbitals, 'pair', axis=0, tiled=True)  53 us
    all_gather x1, waiting for transfers between devices, shards(): chosen = lax.all_gather(picked, 'tm', axis=2, tiled=True)  52.2 us
    dot_general x8, matrix products, shards(): lax.dot_general(left, product, (((0,), (0,)), ((), ())), preferred_elemen...  46.5 us
    dot_general x8, matrix products, shards(): block = jnp.dot(half, right, preferred_element_type=jnp.float32)  23.6 us
    dot_general x8, local copies, waits for them, and re-layouts, shards(): block = jnp.dot(half, right, preferred_element_type=jnp.float32)  17 us
    another operation x3, other arithmetic, shards(): partial_sum = jnp.stack(totals, axis=0)  6.27 us
  transfers between devices with their start and end apart: 3, of which 3 were waited for; matrix products, arithmetic and copies ran while one was open for 1% of the time, Pallas kernels for 0%

commit v1 on v0

v1 whole, which is shorter than its diff:
```python
import functools

import jax
import jax.numpy as jnp
from jax import lax
from jax.experimental import pallas as pl
from jax.experimental.pallas import tpu as pltpu
from jax.sharding import PartitionSpec as P

NOCC = 128
MESH = pl.DeviceIdType.MESH
ROWS = 512


def kernel(
    tm_size, pair_size, pb, gap, orb_in, scr_in, out,
    orb, scr, lt, u, acc, part, rbuf,
    own_sem, scr_sem, ssem, rsem, xs_sem, xr_sem,
):
    times, pairs = scr.shape[0], scr.shape[1]
    points, cols = orb_in.shape
    norb = orb.shape[2]
    half = points // 2
    line = pair_size // 2
    tm = lax.axis_index("tm")
    me = lax.axis_index("pair")
    h, c = tm // 2, tm % 2
    z, y = me // 2, me % 2
    tm_x = (1 - h) * 2 + c
    tm_p = h * 2 + (1 - c)
    me_y = z * 2 + (1 - y)

    barrier = pltpu.get_barrier_semaphore()
    pl.semaphore_signal(barrier, inc=1, device_id=(tm_x, me), device_id_type=MESH)
    pl.semaphore_signal(barrier, inc=1, device_id=(tm_p, me), device_id_type=MESH)
    for k in range(1, pair_size):
        pl.semaphore_signal(
            barrier, inc=1, device_id=(tm, (me + k) % pair_size), device_id_type=MESH
        )

    own_col = pl.ds(pl.multiple_of(tm * cols, cols), cols)
    own = pltpu.make_async_copy(orb_in, orb.at[me, :, own_col], own_sem.at[0])
    own.start()
    pl.semaphore_wait(barrier, pair_size + 1)

    def region(block, column, first=0, count=points):
        return orb.at[
            block, pl.ds(first, count), pl.ds(pl.multiple_of(column * cols, cols), cols)
        ]

    def copy(src, dst, sk, rk, z0, dev):
        return pltpu.make_async_remote_copy(
            src_ref=src, dst_ref=dst, send_sem=ssem.at[sk, z0], recv_sem=rsem.at[rk, z0],
            device_id=dev, device_id_type=MESH,
        )

    def main(z0):
        return region(z0 * 2 + y, tm)

    def c_up(z0, src=None):
        return copy(main(z0) if src is None else src, main(z0), 0, 0, z0, (tm, me + 2))

    def c_down(z0, src=None):
        return copy(main(z0) if src is None else src, main(z0), 1, 0, z0, (tm, me - 2))

    def c_x(z0, src=None):
        return copy(main(z0) if src is None else src, main(z0), 2, 1, z0, (tm_x, me))

    def c_y(z0, src=None):
        return copy(main(z0) if src is None else src, main(z0), 3, 2, z0, (tm, me_y))

    def c_p(z0, src=None):
        return copy(main(z0) if src is None else src, main(z0), 4, 5, z0, (tm_p, me))

    def from_x(z0, *rows):
        return region(z0 * 2 + y, tm_x, *rows)

    def from_y(z0, *rows):
        return region(z0 * 2 + 1 - y, tm, *rows)

    def from_d(z0, *rows):
        return region(z0 * 2 + 1 - y, tm_x, *rows)

    def c_px(z0):
        return copy(from_x(z0), from_x(z0), 5, 6, z0, (tm_p, me))

    def c_py(z0):
        return copy(from_y(z0), from_y(z0), 6, 7, z0, (tm_p, me))

    def c_pd(z0):
        return copy(from_d(z0), from_d(z0), 7, 8, z0, (tm_p, me))

    def c_xy(z0):
        return copy(from_x(z0, 0, half), from_x(z0, 0, half), 8, 3, z0, (tm, me_y))

    def c_yx(z0):
        return copy(from_y(z0, half, half), from_y(z0, half, half), 9, 4, z0, (tm_x, me))

    def arrived(dst, rk, z0):
        copy(dst, dst, 0, rk, z0, (tm_p, me)).wait_recv()

    def guard(cond, f):
        if cond is None:
            f()
        else:
            pl.when(cond)(f)

    groups = [(z, None, 0)]
    for d in range(1, line):
        groups.append((z - d, z - d >= 0, 1))
        groups.append((z + d, z + d < line, 2))

    def stage_a(group):
        z0, cond, way = group

        def body():
            src = orb_in if way == 0 else None
            if way:
                arrived(main(z0), 0, z0)
            if way in (0, 1):
                pl.when(z + 1 < line)(lambda: c_up(z0, src).start())
            if way in (0, 2):
                pl.when(z >= 1)(lambda: c_down(z0, src).start())
            c_x(z0, src).start()
            c_y(z0, src).start()
            c_p(z0, src).start()

        guard(cond, body)

    def stage_b(group):
        z0, cond, way = group

        def body():
            arrived(from_x(z0), 1, z0)
            c_xy(z0).start()
            c_px(z0).start()
            arrived(from_y(z0), 2, z0)
            c_yx(z0).start()
            c_py(z0).start()

        guard(cond, body)

    def stage_c(group):
        z0, cond, way = group

        def body():
            arrived(from_d(z0, 0, half), 3, z0)
            arrived(from_d(z0, half, half), 4, z0)
            c_pd(z0).start()

        guard(cond, body)

    def tile_copy(t, p):
        return pltpu.make_async_copy(scr_in.at[t, p], scr.at[t, p], scr_sem.at[t, p])

    stage_a(groups[0])
    for t in range(times):
        for p in range(pairs):
            tile_copy(t, p).start()
    count = len(groups)
    for k in range(1, count + 2):
        if k < count:
            stage_a(groups[k])
        if 0 <= k - 1 < count:
            stage_b(groups[k - 1])
        if 0 <= k - 2 < count:
            stage_c(groups[k - 2])

    own.wait()
    for z0 in range(line):
        arrived(region(z0 * 2 + y, tm_p), 5, z0)
        other = (1 - h) * 2 + (1 - c)
        arrived(region(z0 * 2 + y, other), 6, z0)
        arrived(region(z0 * 2 + 1 - y, tm_p), 7, z0)
        arrived(region(z0 * 2 + 1 - y, other), 8, z0)
    for z0, cond, way in groups:
        def ends(z0=z0, way=way):
            src = orb_in if way == 0 else None
            if way in (0, 1):
                pl.when(z + 1 < line)(lambda: c_up(z0, src).wait_send())
            if way in (0, 2):
                pl.when(z >= 1)(lambda: c_down(z0, src).wait_send())
            for one in (c_x(z0, src), c_y(z0, src), c_p(z0, src)):
                one.wait_send()
            for one in (c_px(z0), c_py(z0), c_pd(z0), c_xy(z0), c_yx(z0)):
                one.wait_send()

        guard(cond, ends)

    share = out.shape[1]

    def share_copy(t, peer, slot):
        return pltpu.make_async_remote_copy(
            src_ref=part.at[t, pl.ds(pl.multiple_of(peer * share, share), share), :],
            dst_ref=rbuf.at[t, slot],
            send_sem=xs_sem.at[t, peer], recv_sem=xr_sem.at[t, slot],
            device_id=(tm, peer), device_id_type=MESH,
        )

    def peers():
        return [(me + k) % pair_size for k in range(1, pair_size)]

    lane = lax.broadcasted_iota(jnp.int32, (1, norb), 1)
    sign = jnp.where(lane < NOCC, 1.0, -1.0).astype(jnp.float32)
    for t in range(times):
        moment = jnp.full((1, norb), tm * times + t, jnp.int32).astype(jnp.float32)
        tau = 6.0 * (moment + 0.5) / (tm_size * times)
        factor = sign * jnp.exp(-gap[...] * tau)
        acc[...] = jnp.zeros_like(acc)

        def pair_step(p, carry):
            a = pb[p, 0]
            b = pb[p, 1]
            scaled_by = factor * jnp.where(a == b, 0.5, 1.0).astype(jnp.float32)
            tile_copy(t, p).wait()
            for r in range(0, points, ROWS):
                left = orb[a, pl.ds(r, ROWS), :]
                scaled = (left.astype(jnp.float32) * scaled_by).astype(jnp.bfloat16)
                green = lax.dot_general(
                    scaled, orb[b], (((1,), (1,)), ((), ())),
                    preferred_element_type=jnp.float32,
                )
                product = (green * scr[t, p, pl.ds(r, ROWS), :].astype(jnp.float32)).astype(
                    jnp.bfloat16
                )
                u[pl.ds(r, ROWS), :] = jnp.dot(
                    product, orb[b], preferred_element_type=jnp.float32
                ).astype(jnp.bfloat16)
                if t == 0:
                    lt[p, :, pl.ds(r, ROWS)] = left.T
            acc[...] += jnp.dot(lt[p], u[...], preferred_element_type=jnp.float32)
            return carry

        lax.fori_loop(0, pairs, pair_step, 0)
        total = acc[...]
        acc[...] = total + total.T
        part[t] = acc[...].astype(jnp.bfloat16)
        for peer in peers():
            share_copy(t, peer, me).start()
        out[t] = acc[pl.ds(pl.multiple_of(me * share, share), share), :]

    for t in range(times):
        for peer in peers():
            share_copy(t, peer, peer).wait_recv()
        total = out[t]
        for peer in peers():
            total = total + rbuf[t, peer].astype(jnp.float32)
        out[t] = total
    for t in range(times):
        for peer in peers():
            share_copy(t, peer, me).wait_send()


def shards(tm_size, pair_size, orbitals, level_gap, screened, pair_blocks):
    points, cols = orbitals.shape
    times, pairs = screened.shape[:2]
    norb = level_gap.shape[0]
    share = norb // pair_size
    line = pair_size // 2
    bf16, f32 = jnp.bfloat16, jnp.float32
    return pl.pallas_call(
        functools.partial(kernel, tm_size, pair_size),
        out_shape=jax.ShapeDtypeStruct((times, share, norb), f32),
        in_specs=[
            pl.BlockSpec(memory_space=pltpu.SMEM),
            pl.BlockSpec(memory_space=pltpu.VMEM),
            pl.BlockSpec(memory_space=pl.ANY),
            pl.BlockSpec(memory_space=pl.ANY),
        ],
        out_specs=pl.BlockSpec(memory_space=pltpu.VMEM),
        scratch_shapes=[
            pltpu.VMEM((pair_size, points, norb), bf16),
            pltpu.VMEM((times, pairs, points, points), bf16),
            pltpu.VMEM((pairs, norb, points), bf16),
            pltpu.VMEM((points, norb), bf16),
            pltpu.VMEM((norb, norb), f32),
            pltpu.VMEM((times, norb, norb), bf16),
            pltpu.VMEM((times, pair_size, share, norb), bf16),
            pltpu.SemaphoreType.DMA((1,)),
            pltpu.SemaphoreType.DMA((times, pairs)),
            pltpu.SemaphoreType.DMA((10, line)),
            pltpu.SemaphoreType.DMA((9, line)),
            pltpu.SemaphoreType.DMA((times, pair_size)),
            pltpu.SemaphoreType.DMA((times, pair_size)),
        ],
        compiler_params=pltpu.CompilerParams(
            collective_id=0, has_side_effects=True, vmem_limit_bytes=63 * 1024 * 1024
        ),
    )(pair_blocks, level_gap.reshape(1, norb), orbitals, screened)


def solution(mesh):
    return jax.shard_map(
        functools.partial(shards, mesh.shape["tm"], mesh.shape["pair"]),
        mesh=mesh,
        in_specs=(P("pair", "tm"), P(), P("tm", "pair", None, None), P("pair", None)),
        out_specs=P("tm", "pair", None),
        check_vma=False,
    )
```

time: 294 us -> 89.1 us (0.30)
  waiting for transfers between devices: 175 us -> 0 us
  Pallas kernels: 0 us -> 85.9 us
  matrix products: 70.1 us -> 0 us
  local copies, waits for them, and re-layouts: 22.4 us -> 3.01 us
  between operations: 18.3 us -> 0.01 us
  other arithmetic: 8.04 us -> 0 us
    all_gather x2 -> x0, waiting for transfers between devices: 105 us -> none  [the longest x1 53 us: shards(): narrow = lax.all_gather(orbitals, 'pair', axis=0, tiled=True)]
    pallas_call x0 -> x1, Pallas kernels: none -> 85.9 us  [shards(): pl.pallas_call(functools.partial(kernel, tm_size, pair_size), out_shape=j...]
    dot_general x16 -> x0, matrix products: 70.1 us -> none  [the longest x8 46.5 us: shards(): lax.dot_general(left, product, (((0,), (0,)), ((), ())), preferred_elemen...]
    reduce_scatter x1 -> x0, waiting for transfers between devices: 68.9 us -> none  [shards(): lax.psum_scatter(partial_sum, 'pair', scatter_dimension=1, tiled=True)]
    dot_general x8 -> x0, local copies, waits for them, and re-layouts: 17 us -> none  [shards(): block = jnp.dot(half, right, preferred_element_type=jnp.float32)]
    another operation x3 -> x0, other arithmetic: 6.27 us -> none  [shards(): partial_sum = jnp.stack(totals, axis=0)]
  transfers between devices with their start and end apart: 3 -> 0, of which waited for: 3 -> 0; matrix products, arithmetic and copies ran while one was open for 1% -> 0% of each run, Pallas kernels for 0% -> 0%
where the time goes in v1:
time: 89.1 us; the launch traced here: 88.9 us
  Pallas kernels  85.9 us (96%)
  local copies, waits for them, and re-layouts  3.01 us (3%)
    pallas_call x1, Pallas kernels, shards(): pl.pallas_call(functools.partial(kernel, tm_size, pair_size), out_shape=j...  85.9 us
    unnamed x2, local copies, waits for them, and re-layouts  3.01 us

profile of v1, /device:TPU:0, one launch (start us, length us, event | category | flops | bytes accessed | tf_op | source)
XLA Modules:
  0.0 88.9 jit_solution(2004754074576262424)
XLA Ops:
  0.0 1.3 %copy.5.pb = s32[4,2]{1,0:T(4,128)} copy(s32[4,2]{0,1:T(2,128)} %param.7) | data formatting | bytes 64 | tf_op args[3]
  1.3 85.9 %shard_map.46 = f32[2,64,512]{2,1,0:T(8,128)} custom-call(s32[4,2]{1,0:T(4,128)} %copy.5.pb, f32[1,512]{1,0:T(1,128)} %bitcast.1, bf16[1024,128]{1,0:T(8,128)(2,1)} %orb_in.1, bf16[2,4,1024,1024]{3,2,1,0:T(8,128)(2,1)} %scr_in.1), custom_call_target="tpu_custom_call" | custom-call | tf_op jit(solution)/shard_map/pallas_call | solution.py:261
  87.2 1.7 %copy.7 = f32[2,64,512]{2,1,0:T(8,128)} copy(f32[2,64,512]{2,1,0:T(8,128)} %shard_map.46) | data formatting | bytes 524288

commit v2 on v1

--- a/solution.py
+++ b/solution.py
@@ -14,13 +14,13 @@
 
 def kernel(
     tm_size, pair_size, pb, gap, orb_in, scr_in, out,
-    orb, scr, lt, u, acc, part, rbuf,
+    orb, scr, lt, u, acc, part, rbuf, zpart,
     own_sem, scr_sem, ssem, rsem, xs_sem, xr_sem,
 ):
     times, pairs = scr.shape[0], scr.shape[1]
     points, cols = orb_in.shape
     norb = orb.shape[2]
-    half = points // 2
+    half, quarter = points // 2, points // 4
     line = pair_size // 2
     tm = lax.axis_index("tm")
     me = lax.axis_index("pair")
@@ -33,15 +33,21 @@
     barrier = pltpu.get_barrier_semaphore()
     pl.semaphore_signal(barrier, inc=1, device_id=(tm_x, me), device_id_type=MESH)
     pl.semaphore_signal(barrier, inc=1, device_id=(tm_p, me), device_id_type=MESH)
-    for k in range(1, pair_size):
-        pl.semaphore_signal(
-            barrier, inc=1, device_id=(tm, (me + k) % pair_size), device_id_type=MESH
-        )
+    pl.semaphore_signal(barrier, inc=1, device_id=(tm, me_y), device_id_type=MESH)
+
+    @pl.when(z >= 1)
+    def _():
+        pl.semaphore_signal(barrier, inc=1, device_id=(tm, me - 2), device_id_type=MESH)
+
+    @pl.when(z + 1 < line)
+    def _():
+        pl.semaphore_signal(barrier, inc=1, device_id=(tm, me + 2), device_id_type=MESH)
 
     own_col = pl.ds(pl.multiple_of(tm * cols, cols), cols)
     own = pltpu.make_async_copy(orb_in, orb.at[me, :, own_col], own_sem.at[0])
     own.start()
-    pl.semaphore_wait(barrier, pair_size + 1)
+    along = (z + line - 1) // line + (2 * line - 2 - z) // line
+    pl.semaphore_wait(barrier, 3 + along)
 
     def region(block, column, first=0, count=points):
         return orb.at[
@@ -90,11 +96,27 @@
     def c_pd(z0):
         return copy(from_d(z0), from_d(z0), 7, 8, z0, (tm_p, me))
 
-    def c_xy(z0):
-        return copy(from_x(z0, 0, half), from_x(z0, 0, half), 8, 3, z0, (tm, me_y))
-
-    def c_yx(z0):
-        return copy(from_y(z0, half, half), from_y(z0, half, half), 9, 4, z0, (tm_x, me))
+    def rows_xy(way):
+        return (0, quarter) if way else (0, half)
+
+    def rows_yx(way):
+        return (quarter, quarter) if way else (half, half)
+
+    def c_xy(z0, way):
+        rows = from_x(z0, *rows_xy(way))
+        return copy(rows, rows, 8, 3, z0, (tm, me_y))
+
+    def c_yx(z0, way):
+        rows = from_y(z0, *rows_yx(way))
+        return copy(rows, rows, 9, 4, z0, (tm_x, me))
+
+    def c_dup(z0):
+        rows = from_d(z0, half, half)
+        return copy(rows, rows, 10, 9, z0, (tm, me + 2))
+
+    def c_ddown(z0):
+        rows = from_d(z0, half, half)
+        return copy(rows, rows, 11, 9, z0, (tm, me - 2))
 
     def arrived(dst, rk, z0):
         copy(dst, dst, 0, rk, z0, (tm_p, me)).wait_recv()
@@ -132,10 +154,10 @@
 
         def body():
             arrived(from_x(z0), 1, z0)
-            c_xy(z0).start()
+            c_xy(z0, way).start()
             c_px(z0).start()
             arrived(from_y(z0), 2, z0)
-            c_yx(z0).start()
+            c_yx(z0, way).start()
             c_py(z0).start()
 
         guard(cond, body)
@@ -144,9 +166,24 @@
         z0, cond, way = group
 
         def body():
-            arrived(from_d(z0, 0, half), 3, z0)
-            arrived(from_d(z0, half, half), 4, z0)
+            arrived(from_d(z0, *rows_xy(way)), 3, z0)
+            arrived(from_d(z0, *rows_yx(way)), 4, z0)
+            if way == 0:
+                pl.when(z + 1 < line)(lambda: c_dup(z0).start())
+                pl.when(z >= 1)(lambda: c_ddown(z0).start())
             c_pd(z0).start()
+
+        guard(cond, body)
+
+    def stage_r(group):
+        z0, cond, way = group
+
+        def body():
+            arrived(from_d(z0, half, half), 9, z0)
+            if way == 1:
+                pl.when(z + 1 < line)(lambda: c_dup(z0).start())
+            else:
+                pl.when(z >= 1)(lambda: c_ddown(z0).start())
 
         guard(cond, body)
 
@@ -158,13 +195,22 @@
         for p in range(pairs):
             tile_copy(t, p).start()
     count = len(groups)
-    for k in range(1, count + 2):
+    for k in range(1, count + 3):
         if k < count:
             stage_a(groups[k])
-        if 0 <= k - 1 < count:
-            stage_b(groups[k - 1])
-        if 0 <= k - 2 < count:
-            stage_c(groups[k - 2])
+        if k == 1:
+            pl.when(z >= 1)(lambda: stage_b(groups[0]))
+        if k == 2:
+            pl.when(z == 0)(lambda: stage_b(groups[0]))
+        if k == 4:
+            stage_c(groups[0])
+        if 1 <= k - 3 < count:
+            stage_r(groups[k - 3])
+            stage_b(groups[k - 3])
+        if 1 <= k - 6 < count:
+            stage_c(groups[k - 6])
+    for group in groups[max(1, count - 3):]:
+        stage_c(group)
 
     own.wait()
     for z0 in range(line):
@@ -176,13 +222,21 @@
     for z0, cond, way in groups:
         def ends(z0=z0, way=way):
             src = orb_in if way == 0 else None
+            def up():
+                c_up(z0, src).wait_send()
+                c_dup(z0).wait_send()
+
+            def down():
+                c_down(z0, src).wait_send()
+                c_ddown(z0).wait_send()
+
             if way in (0, 1):
-                pl.when(z + 1 < line)(lambda: c_up(z0, src).wait_send())
+                pl.when(z + 1 < line)(up)
             if way in (0, 2):
-                pl.when(z >= 1)(lambda: c_down(z0, src).wait_send())
+                pl.when(z >= 1)(down)
             for one in (c_x(z0, src), c_y(z0, src), c_p(z0, src)):
                 one.wait_send()
-            for one in (c_px(z0), c_py(z0), c_pd(z0), c_xy(z0), c_yx(z0)):
+            for one in (c_px(z0), c_py(z0), c_pd(z0), c_xy(z0, way), c_yx(z0, way)):
                 one.wait_send()
 
         guard(cond, ends)
@@ -200,6 +254,26 @@
     def peers():
         return [(me + k) % pair_size for k in range(1, pair_size)]
 
+    def far():
+        return [(z + k) % line for k in range(1, line)] + [z]
+
+    def y_copy(z1):
+        peer = z1 * 2 + 1 - y
+        return pltpu.make_async_remote_copy(
+            src_ref=part.at[times - 1, pl.ds(pl.multiple_of(peer * share, share), share), :],
+            dst_ref=rbuf.at[times - 1, z1 * 2],
+            send_sem=xs_sem.at[times - 1, z1 * 2], recv_sem=xr_sem.at[times - 1, z1 * 2],
+            device_id=(tm, me_y), device_id_type=MESH,
+        )
+
+    def z_copy(z1, slot):
+        return pltpu.make_async_remote_copy(
+            src_ref=zpart.at[z1], dst_ref=rbuf.at[times - 1, slot * 2 + 1],
+            send_sem=xs_sem.at[times - 1, z1 * 2 + 1],
+            recv_sem=xr_sem.at[times - 1, slot * 2 + 1],
+            device_id=(tm, z1 * 2 + y), device_id_type=MESH,
+        )
+
     lane = lax.broadcasted_iota(jnp.int32, (1, norb), 1)
     sign = jnp.where(lane < NOCC, 1.0, -1.0).astype(jnp.float32)
     for t in range(times):
@@ -209,8 +283,8 @@
         acc[...] = jnp.zeros_like(acc)
 
         def pair_step(p, carry):
-            a = pb[p, 0]
-            b = pb[p, 1]
+            a = pb[0, p]
+            b = pb[1, p]
             scaled_by = factor * jnp.where(a == b, 0.5, 1.0).astype(jnp.float32)
             tile_copy(t, p).wait()
             for r in range(0, points, ROWS):
@@ -235,20 +309,41 @@
         total = acc[...]
         acc[...] = total + total.T
         part[t] = acc[...].astype(jnp.bfloat16)
-        for peer in peers():
-            share_copy(t, peer, me).start()
+        if t < times - 1:
+            for peer in peers():
+                share_copy(t, peer, me).start()
+        else:
+            for z1 in far():
+                y_copy(z1).start()
         out[t] = acc[pl.ds(pl.multiple_of(me * share, share), share), :]
 
-    for t in range(times):
+    t = times - 1
+    for z1 in far()[:-1]:
+        y_copy(z1).wait_recv()
+        rows = acc[pl.ds(pl.multiple_of((z1 * 2 + y) * share, share), share), :]
+        zpart[z1] = (rows + rbuf[t, z1 * 2].astype(jnp.float32)).astype(jnp.bfloat16)
+        z_copy(z1, z).start()
+    for t in range(times - 1):
         for peer in peers():
             share_copy(t, peer, peer).wait_recv()
         total = out[t]
         for peer in peers():
             total = total + rbuf[t, peer].astype(jnp.float32)
         out[t] = total
-    for t in range(times):
+    t = times - 1
+    y_copy(z).wait_recv()
+    total = out[t] + rbuf[t, z * 2].astype(jnp.float32)
+    for z1 in far()[:-1]:
+        z_copy(z1, z1).wait_recv()
+        total = total + rbuf[t, z1 * 2 + 1].astype(jnp.float32)
+    out[t] = total
+    for t in range(times - 1):
         for peer in peers():
             share_copy(t, peer, me).wait_send()
+    for z1 in far():
+        y_copy(z1).wait_send()
+    for z1 in far()[:-1]:
+        z_copy(z1, z).wait_send()
 
 
 def shards(tm_size, pair_size, orbitals, level_gap, screened, pair_blocks):
@@ -276,17 +371,18 @@
             pltpu.VMEM((norb, norb), f32),
             pltpu.VMEM((times, norb, norb), bf16),
             pltpu.VMEM((times, pair_size, share, norb), bf16),
+            pltpu.VMEM((line, share, norb), bf16),
             pltpu.SemaphoreType.DMA((1,)),
             pltpu.SemaphoreType.DMA((times, pairs)),
+            pltpu.SemaphoreType.DMA((12, line)),
             pltpu.SemaphoreType.DMA((10, line)),
-            pltpu.SemaphoreType.DMA((9, line)),
             pltpu.SemaphoreType.DMA((times, pair_size)),
             pltpu.SemaphoreType.DMA((times, pair_size)),
         ],
         compiler_params=pltpu.CompilerParams(
             collective_id=0, has_side_effects=True, vmem_limit_bytes=63 * 1024 * 1024
         ),
-    )(pair_blocks, level_gap.reshape(1, norb), orbitals, screened)
+    )(pair_blocks.T, level_gap.reshape(1, norb), orbitals, screened)
 
 
 def solution(mesh):

time: 89.1 us -> 79 us (0.89)
  Pallas kernels: 85.9 us -> 77.1 us
  local copies, waits for them, and re-layouts: 3.01 us -> 1.67 us
    pallas_call x1, Pallas kernels: 85.9 us -> 77.1 us  [shards(): pl.pallas_call(functools.partial(kernel, tm_size, pair_size), out_shape=j...]
    unnamed x2 -> x1, local copies, waits for them, and re-layouts: 3.01 us -> 1.67 us
where the time goes in v2:
time: 79 us; the launch traced here: 78.8 us
  Pallas kernels  77.1 us (98%)
  local copies, waits for them, and re-layouts  1.67 us (2%)
    pallas_call x1, Pallas kernels, shards(): pl.pallas_call(functools.partial(kernel, tm_size, pair_size), out_shape=j...  77.1 us
    unnamed x1, local copies, waits for them, and re-layouts  1.67 us

profile of v2, /device:TPU:0, one launch (start us, length us, event | category | flops | bytes accessed | tf_op | source)
XLA Modules:
  0.0 78.8 jit_solution(17457834981021107499)
XLA Ops:
  0.0 77.1 %shard_map.46 = f32[2,64,512]{2,1,0:T(8,128)} custom-call(s32[2,4]{1,0:T(2,128)} %bitcast.3, f32[1,512]{1,0:T(1,128)} %bitcast.2, bf16[1024,128]{1,0:T(8,128)(2,1)} %orb_in.1, bf16[2,4,1024,1024]{3,2,1,0:T(8,128)(2,1)} %scr_in.1), custom_call_target="tpu_custom_call" | custom-call | tf_op jit(solution)/shard_map/pallas_call | solution.py:356
  77.1 1.7 %copy.6 = f32[2,64,512]{2,1,0:T(8,128)} copy(f32[2,64,512]{2,1,0:T(8,128)} %shard_map.46) | data formatting | bytes 524288
